TPU v7x, 512 devices: a whole 4x8x8 slice. The times are simulated.
512 devices in a mesh: dp: 64 (over z_hi, y, core), rows: 8 (over z_lo, x).
Axes of the slice: x: 4, y: 8, z: 8 (z_hi: 4, z_lo: 2; z = z_hi * 2 + z_lo), core: 2. Of those that a mesh axis runs over, the one named last changes fastest.
Arguments:
- latents: bfloat16 [64, 32, 32, 640], P('dp', 'rows'), may hold values from -6 to 6
- target: bfloat16 [64, 32, 32, 640], P('dp', 'rows'), may hold values from -6 to 6
- weight: float32 [9, 640, 640], P(None, 'rows', 'dp'), may hold values from -0.078125 to 0.078125
- moment1: float32 [9, 640, 640], P(None, 'rows', 'dp'), may hold values from -6 to 6
- moment2: float32 [9, 640, 640], P(None, 'rows', 'dp'), may hold values from 0.5 to 4
Outputs:
- student: bfloat16 [64, 32, 32, 640], P('dp', 'rows')
- input_grad: bfloat16 [64, 32, 32, 640], P('dp', 'rows')
- new_weight: float32 [9, 640, 640], P(None, 'rows', 'dp')
- new_moment1: float32 [9, 640, 640], P(None, 'rows', 'dp')
- new_moment2: float32 [9, 640, 640], P(None, 'rows', 'dp')
All inputs are finite; a program needn't handle non-finite values.
Results may differ from a plain program's by a relative error of at most 0.009.
Values may be sent and summed in bfloat16 or wider, within the bound.
A program may use at most 128 MiB of HBM per device.

v0:
```python
import jax
import jax.numpy as jnp
from jax import lax
from jax.sharding import PartitionSpec as P


def per_device(latents, target, weight, moment1, moment2):
    n_rows = lax.axis_size("rows")
    n_dp = lax.axis_size("dp")
    batch, band, width, ch = latents.shape
    taps, cs, ns = weight.shape
    height = band * n_rows
    cells = batch * band * width
    own = weight.astype(jnp.bfloat16).transpose(2, 0, 1).reshape(ns, taps * cs)
    kernel = lax.all_gather(own, "dp", axis=0, tiled=True)
    x = lax.all_to_all(latents, "rows", split_axis=3, concat_axis=1, tiled=True)
    pad = jnp.pad(x, ((0, 0), (1, 1), (1, 1), (0, 0)))
    wins = [pad[:, a : a + height, c : c + width] for a in range(3) for c in range(3)]
    x9 = jnp.concatenate(wins, axis=-1).reshape(batch * height * width, taps * cs)
    part = lax.dot_general(x9, kernel, (((1,), (1,)), ((), ())), preferred_element_type=jnp.float32)
    part = part.astype(jnp.bfloat16).reshape(batch, n_rows, band * width, ch)
    part = part.transpose(1, 0, 2, 3).reshape(n_rows, cells, ch)
    part = lax.all_to_all(part, "rows", 0, 0, tiled=True)
    student = jnp.sum(part.astype(jnp.float32), axis=0).astype(jnp.bfloat16)
    error = student.astype(jnp.float32) - target.reshape(cells, ch).astype(jnp.float32)
    error = error.astype(jnp.bfloat16).reshape(batch, band, width, ch)
    err = lax.all_gather(error, "rows", axis=1, tiled=True).reshape(-1, ch)
    grad = lax.dot_general(err, x9, (((0,), (0,)), ((), ())), preferred_element_type=jnp.float32)
    grad = grad.astype(jnp.bfloat16).reshape(n_dp, ns, taps * cs)
    grad = lax.all_to_all(grad, "dp", 0, 0, tiled=True)
    grad = jnp.sum(grad.astype(jnp.float32), axis=0) / jnp.float32(batch * n_dp)
    grad = grad.reshape(ns, taps, cs).transpose(1, 2, 0)
    back = jnp.dot(err, kernel, preferred_element_type=jnp.float32)
    back = back.reshape(batch, height, width, taps, cs)
    back = jnp.pad(back, ((0, 0), (1, 1), (1, 1), (0, 0), (0, 0)))
    total = None
    for tap in range(taps):
        a, c = divmod(tap, 3)
        term = back[:, 2 - a : 2 - a + height, 2 - c : 2 - c + width, tap]
        total = term if total is None else total + term
    input_grad = lax.all_to_all(
        total.astype(jnp.bfloat16), "rows", split_axis=1, concat_axis=3, tiled=True
    )
    new_moment1 = 0.9 * moment1 + 0.1 * grad
    new_moment2 = 0.999 * moment2 + 0.001 * grad * grad
    new_weight = weight - 0.01 * new_moment1 / (jnp.sqrt(new_moment2) + 1e-08)
    return (student.reshape(latents.shape), input_grad, new_weight, new_moment1, new_moment2)


def solution(mesh):
    act = P("dp", "rows", None, None)
    par = P(None, "rows", "dp")
    return jax.shard_map(
        per_device,
        mesh=mesh,
        in_specs=(act, act, par, par, par),
        out_specs=(act, act, par, par, par),
        check_vma=False,
    )
```

profile of v0, /device:TPU:1, one launch (start us, length us, event | category | flops | bytes accessed | tf_op | source)
XLA Modules:
  0.0 255.2 jit_solution(7276642183336504303)
XLA Ops:
  7.2 0.0 copy-start.13
  7.2 1.3 copy.23
  8.5 1.3 reshape.187
  9.8 6.6 %all-to-all-start = ((bf16[8,2,5120]{2,1,0:T(2,128)(2,1)}), bf16[8,2,5120]{2,1,0:T(2,128)(2,1)S(1)}, u32[]{:S(2)}, u32[]{:S(2)}) async-start(bf16[8,2,5120]{2,1,0:T(2,128)(2,1)} %reshape.187), calls=%async_computation | async-start | bytes 327680 | tf_op jit(solution)/shard_map/all_to_all | solution.py:16
  16.4 0.0 all-gather.3.cloned.1.call-start
  16.5 0.0 copy-done.13
  16.5 0.1 reshape.181
  16.6 92.6 %all-gather = bf16[64,10,720]{2,1,0:T(8,128)(2,1)S(1)} all-gather(bf16[1,10,720]{2,1,0:T(8,128)(2,1)S(1)} %reshape.181), channel_id=1, replica_groups=mesh['dp'=64,'rows'=8] {'dp'}, dimensions={0}, use_global_device_ids=true | all-gather | bytes 936000 | tf_op jit(solution)/shard_map/all_gather | solution.py:15
  109.2 0.6 reshape.182
  109.8 0.0 all-to-all-done
  109.8 0.3 reshape.188
  110.2 0.3 copy.24
  110.5 0.3 pad_slice_fusion.8
  110.8 0.0 copy-start
  110.8 0.0 copy-start.2
  110.8 0.0 copy-start.4
  110.8 0.0 copy-start.6
  110.9 0.0 copy-start.8
  110.9 2.4 concatenate.33
  113.3 0.0 copy-done
  113.3 0.0 copy-done.2
  113.3 0.0 copy-done.4
  113.3 0.0 copy-done.6
  113.3 0.0 copy-done.8
  113.3 2.8 %convolution_convert_fusion = bf16[1024,640]{1,0:T(8,128)(2,1)S(1)} fusion(bf16[1024,720]{1,0:T(8,128)(2,1)} %concatenate.33, bf16[640,720]{1,0:T(8,128)(2,1)S(1)} %reshape.182), kind=kOutput, calls=%fused_computation.11 | convolution fusion | flops 944373760 | bytes 3706880 | tf_op jit(solution)/shard_map/dot_general | solution.py:20
  116.2 23.0 %all_to_all.46 = bf16[8,128,640]{2,1,0:T(8,128)(2,1)S(1)} all-to-all(bf16[8,128,640]{2,1,0:T(8,128)(2,1)S(1)} %bitcast.78), channel_id=1, replica_groups=mesh['dp'=64,'rows'=8] {'rows'}, dimensions={0} | all-to-all | bytes 2621440 | tf_op jit(solution)/shard_map/all_to_all | solution.py:23
  139.2 0.2 reduce_sum.21
  139.4 0.0 copy-start.12
  139.4 0.0 copy-start.1
  139.4 0.0 copy-start.3
  139.4 0.0 copy-start.5
  139.4 0.0 copy-start.7
  139.4 0.0 copy-start.9
  139.4 1.7 subtract_convert_fusion
  141.2 0.0 all-gather.3.cloned.1.call-update
  141.2 1.3 copy.27
  142.5 0.0 copy-done.1
  142.5 0.0 copy-done.3
  142.5 0.0 copy-done.5
  142.5 0.0 copy-done.7
  142.6 0.0 copy-done.9
  142.6 0.0 copy-start.11
  142.6 2.4 concatenate.34
  145.0 26.3 %all-gather.3.cloned.1.call-done = bf16[1,32,32,640]{3,2,0,1:T(8,128)(2,1)} async-done(((bf16[1,4,32,640]{3,2,0,1:T(8,128)(2,1)}), bf16[1,32,32,640]{3,2,0,1:T(8,128)(2,1)}) %all-gather.3.cloned.1.call-update) | async-done | bytes 1310736 | tf_op jit(solution)/shard_map/all_gather | solution.py:27
  171.3 3.5 %convolution_bitcast_fusion = f32[1,32,32,9,80]{4,2,3,1,0:T(8,128)S(1)} fusion(bf16[9,80,640,1]{2,1,0,3:T(8,128)(2,1)S(1)} %bitcast.80, bf16[1,32,32,640]{3,2,0,1:T(8,128)(2,1)} %all-gather.3.cloned.1.call-done), kind=kOutput, calls=%fused_computation.9 | convolution fusion | flops 943718400 | bytes 5181440 | tf_op jit(solution)/shard_map/dot_general | solution.py:33
  174.8 1.3 fusion.15
  176.1 3.4 %all-to-all-start.2 = ((bf16[1,32,32,80]{3,2,0,1:T(8,128)(2,1)}), bf16[1,32,32,80]{3,2,0,1:T(8,128)(2,1)S(1)}, u32[]{:S(2)}, u32[]{:S(2)}) async-start(bf16[1,32,32,80]{3,2,0,1:T(8,128)(2,1)} %fusion.15), calls=%async_computation.2 | async-start | bytes 524288 | tf_op jit(solution)/shard_map/all_to_all | solution.py:41
  179.5 2.7 %bitcast_convert_fusion = bf16[640,720]{0,1:T(8,128)(2,1)S(1)} fusion(bf16[1,32,32,720]{3,2,1,0:T(8,128)(2,1)S(1)} %copy-done.10, bf16[1,32,32,640]{3,2,0,1:T(8,128)(2,1)} %all-gather.3.cloned.1.call-done), kind=kOutput, calls=%fused_computation.10 | convolution fusion | flops 944179200 | bytes 3706880 | tf_op jit(solution)/shard_map/dot_general | solution.py:28
  182.2 1.0 copy.31
  183.2 1.4 reshape.175
  184.6 1.0 all-to-all-done.2
  185.6 19.8 %all-to-all-start.3 = ((bf16[64,10,720]{2,1,0:T(8,128)(2,1)}), bf16[64,10,720]{2,1,0:T(8,128)(2,1)S(1)}, u32[]{:S(2)}, u32[]{:S(2)}) async-start(bf16[64,10,720]{2,1,0:T(8,128)(2,1)} %reshape.175), calls=%async_computation.3 | async-start | bytes 3145728 | tf_op jit(solution)/shard_map/all_to_all | solution.py:30
  205.4 0.0 copy-start.14
  205.4 0.0 copy-start.15
  205.4 0.0 copy-start.16
  205.4 0.2 copy.29
  205.6 0.9 all_to_all.40
  206.5 39.4 %all-to-all-done.3 = bf16[64,10,720]{2,1,0:T(8,128)(2,1)S(1)} async-done(((bf16[64,10,720]{2,1,0:T(8,128)(2,1)}), bf16[64,10,720]{2,1,0:T(8,128)(2,1)S(1)}, u32[]{:S(2)}, u32[]{:S(2)}) %all-to-all-start.3) | async-done | bytes 921632 | tf_op jit(solution)/shard_map/all_to_all | solution.py:30
  245.9 0.3 convert_reduce_fusion
  246.2 0.1 div.13
  246.3 0.1 copy_subtract_fusion
  246.4 0.6 copy.35
  247.0 0.6 copy.36
  247.7 0.6 copy.37
  (10 shorter events, 0.0 us)
Async XLA Ops:
  7.2 9.3 %copy-start.13 = (f32[9,80,10]{1,2,0:T(8,128)S(1)}, f32[9,80,10]{1,2,0:T(8,128)}, u32[]{:S(2)}) copy-start(f32[9,80,10]{1,2,0:T(8,128)} %param.7) | copy-start | bytes 86404
  9.8 100.0 %all-to-all-start = ((bf16[8,2,5120]{2,1,0:T(2,128)(2,1)}), bf16[8,2,5120]{2,1,0:T(2,128)(2,1)S(1)}, u32[]{:S(2)}, u32[]{:S(2)}) async-start(bf16[8,2,5120]{2,1,0:T(2,128)(2,1)} %reshape.187), calls=%async_computation | async-start | bytes 327680 | tf_op jit(solution)/shard_map/all_to_all | solution.py:16
  16.4 154.8 %all-gather.3.cloned.1.call-start = ((), (), s32[]{:S(2)}) async-start(), calls=%async_computation.4 | async-start | bytes 1474560 | tf_op jit(solution)/shard_map/all_gather | solution.py:27
  110.8 2.5 copy-start
  110.8 2.5 copy-start.2
  110.8 2.5 copy-start.4
  110.8 2.5 copy-start.6
  110.9 2.5 copy-start.8
  139.4 5.6 %copy-start.12 = (bf16[128,640]{1,0:T(8,128)(2,1)}, bf16[128,640]{1,0:T(8,128)(2,1)S(1)}, u32[]{:S(2)}) copy-start(bf16[128,640]{1,0:T(8,128)(2,1)S(1)} %reduce_sum.21) | copy-start | bytes 491524
  139.4 3.1 %copy-start.1 = (bf16[1,32,32,80]{3,2,1,0:T(8,128)(2,1)S(1)}, bf16[1,32,32,80]{3,2,1,0:T(8,128)(2,1)}, u32[]{:S(2)}) copy-start(bf16[1,32,32,80]{3,2,1,0:T(8,128)(2,1)} %copy-done) | copy-start | bytes 491524
  139.4 3.1 %copy-start.3 = (bf16[1,32,32,80]{3,2,1,0:T(8,128)(2,1)S(1)}, bf16[1,32,32,80]{3,2,1,0:T(8,128)(2,1)}, u32[]{:S(2)}) copy-start(bf16[1,32,32,80]{3,2,1,0:T(8,128)(2,1)} %copy-done.2) | copy-start | bytes 491524
  139.4 3.1 %copy-start.5 = (bf16[1,32,32,80]{3,2,1,0:T(8,128)(2,1)S(1)}, bf16[1,32,32,80]{3,2,1,0:T(8,128)(2,1)}, u32[]{:S(2)}) copy-start(bf16[1,32,32,80]{3,2,1,0:T(8,128)(2,1)} %copy-done.4) | copy-start | bytes 491524
  139.4 3.1 %copy-start.7 = (bf16[1,32,32,80]{3,2,1,0:T(8,128)(2,1)S(1)}, bf16[1,32,32,80]{3,2,1,0:T(8,128)(2,1)}, u32[]{:S(2)}) copy-start(bf16[1,32,32,80]{3,2,1,0:T(8,128)(2,1)} %copy-done.6) | copy-start | bytes 491524
  139.4 3.1 %copy-start.9 = (bf16[1,32,32,80]{3,2,1,0:T(8,128)(2,1)S(1)}, bf16[1,32,32,80]{3,2,1,0:T(8,128)(2,1)}, u32[]{:S(2)}) copy-start(bf16[1,32,32,80]{3,2,1,0:T(8,128)(2,1)} %copy-done.8) | copy-start | bytes 491524
  142.6 28.7 %copy-start.11 = (bf16[720,640]{1,0:T(8,128)(2,1)S(1)}, bf16[720,640]{1,0:T(8,128)(2,1)}, u32[]{:S(2)}) copy-start(bf16[720,640]{1,0:T(8,128)(2,1)} %copy.27) | copy-start | bytes 2764804
  174.8 4.7 %copy-start.10 = (bf16[1,32,32,720]{3,2,1,0:T(8,128)(2,1)S(1)}, bf16[1,32,32,720]{3,2,1,0:T(8,128)(2,1)}, u32[]{:S(2)}) copy-start(bf16[1,32,32,720]{3,2,1,0:T(8,128)(2,1)} %concatenate.34) | copy-start | bytes 4423684
  176.1 9.5 %all-to-all-start.2 = ((bf16[1,32,32,80]{3,2,0,1:T(8,128)(2,1)}), bf16[1,32,32,80]{3,2,0,1:T(8,128)(2,1)S(1)}, u32[]{:S(2)}, u32[]{:S(2)}) async-start(bf16[1,32,32,80]{3,2,0,1:T(8,128)(2,1)} %fusion.15), calls=%async_computation.2 | async-start | bytes 524288 | tf_op jit(solution)/shard_map/all_to_all | solution.py:41
  185.6 60.3 %all-to-all-start.3 = ((bf16[64,10,720]{2,1,0:T(8,128)(2,1)}), bf16[64,10,720]{2,1,0:T(8,128)(2,1)S(1)}, u32[]{:S(2)}, u32[]{:S(2)}) async-start(bf16[64,10,720]{2,1,0:T(8,128)(2,1)} %reshape.175), calls=%async_computation.3 | async-start | bytes 3145728 | tf_op jit(solution)/shard_map/all_to_all | solution.py:30
  205.4 40.9 %copy-start.14 = (f32[9,80,10]{1,2,0:T(8,128)S(1)}, f32[9,80,10]{1,2,0:T(8,128)}, u32[]{:S(2)}) copy-start(f32[9,80,10]{1,2,0:T(8,128)} %param.7) | copy-start | bytes 86404
  205.4 40.9 %copy-start.15 = (f32[9,80,10]{1,2,0:T(8,128)S(1)}, f32[9,80,10]{1,2,0:T(8,128)}, u32[]{:S(2)}) copy-start(f32[9,80,10]{1,2,0:T(8,128)} %param.8) | copy-start | bytes 86404
  205.4 40.9 %copy-start.16 = (f32[9,80,10]{1,2,0:T(8,128)S(1)}, f32[9,80,10]{1,2,0:T(8,128)}, u32[]{:S(2)}) copy-start(f32[9,80,10]{1,2,0:T(8,128)} %param.9) | copy-start | bytes 86404
Sparse Core Ops, SparseCore 0:
  141.3 29.9 all-gather.2
where the time goes:
time: 256 us; the launch traced here: 255 us
  blocking collectives  116 us (45%)
  waiting for transfers between devices  66.7 us (26%)
  starting transfers between devices  29.9 us (12%)
  local copies, waits for them, and re-layouts  16 us (6%)
  between operations  14.4 us (6%)
  matrix products  8.98 us (4%)
  other arithmetic  3.59 us (1%)
    all_gather x1, blocking collectives, per_device(): kernel = lax.all_gather(own, 'dp', axis=0, tiled=True)  92.6 us
    all_to_all x1, waiting for transfers between devices, per_device(): grad = lax.all_to_all(grad, 'dp', 0, 0, tiled=True)  39.4 us
    all_gather x1, waiting for transfers between devices, per_device(): err = lax.all_gather(error, 'rows', axis=1, tiled=True).reshape(-1, ch)  26.3 us
    all_to_all x1, blocking collectives, per_device(): part = lax.all_to_all(part, 'rows', 0, 0, tiled=True)  23 us
    all_to_all x1, starting transfers between devices, per_device(): grad = lax.all_to_all(grad, 'dp', 0, 0, tiled=True)  19.8 us
    all_to_all x1, starting transfers between devices, per_device(): x = lax.all_to_all(latents, 'rows', split_axis=3, concat_axis=1, tiled=True)  6.65 us
    unnamed x42, local copies, waits for them, and re-layouts  5.67 us
  transfers between devices with their start and end apart: 4, of which 3 were waited for; matrix products, arithmetic and copies ran while one was open for 4% of the time, Pallas kernels for 0%

commit v1 on v0

--- a/solution.py
+++ b/solution.py
@@ -24,7 +24,9 @@
     student = jnp.sum(part.astype(jnp.float32), axis=0).astype(jnp.bfloat16)
     error = student.astype(jnp.float32) - target.reshape(cells, ch).astype(jnp.float32)
     error = error.astype(jnp.bfloat16).reshape(batch, band, width, ch)
-    err = lax.all_gather(error, "rows", axis=1, tiled=True).reshape(-1, ch)
+    err = jnp.concatenate(
+        lax.all_to_all(jnp.stack([error] * lax.axis_size("rows")), "rows", 0, 0), axis=1
+    ).reshape(-1, ch)
     grad = lax.dot_general(err, x9, (((0,), (0,)), ((), ())), preferred_element_type=jnp.float32)
     grad = grad.astype(jnp.bfloat16).reshape(n_dp, ns, taps * cs)
     grad = lax.all_to_all(grad, "dp", 0, 0, tiled=True)

time: 256 us -> 221 us (0.86)
  between operations: 14.4 us -> 0.86 us
  waiting for transfers between devices: 66.7 us -> 57 us
  starting transfers between devices: 29.9 us -> 20.5 us
    all_gather x1 -> x0, waiting for transfers between devices: 26.3 us -> none  [per_device(): err = lax.all_gather(error, 'rows', axis=1, tiled=True).reshape(-1, ch)]
    all_to_all x0 -> x1, waiting for transfers between devices: none -> 16.5 us  [per_device(): lax.all_to_all(jnp.stack([error] * lax.axis_size('rows')), 'rows', 0, 0)]
    all_to_all x1, starting transfers between devices: 19.8 us -> 6.1 us  [per_device(): grad = lax.all_to_all(grad, 'dp', 0, 0, tiled=True)]
    all_to_all x0 -> x1, starting transfers between devices: none -> 4.15 us  [per_device(): lax.all_to_all(jnp.stack([error] * lax.axis_size('rows')), 'rows', 0, 0)]
    unnamed x42 -> x22, local copies, waits for them, and re-layouts: 5.67 us -> 5.62 us
  transfers between devices with their start and end apart: 4 -> 4, of which waited for: 3 -> 3; matrix products, arithmetic and copies ran while one was open for 4% -> 3% of each run, Pallas kernels for 0% -> 0%
where the time goes in v1:
time: 221 us; the launch traced here: 220 us
  blocking collectives  116 us (52%)
  waiting for transfers between devices  57 us (26%)
  starting transfers between devices  20.5 us (9%)
  local copies, waits for them, and re-layouts  16.9 us (8%)
  matrix products  7.04 us (3%)
    all_gather x1, blocking collectives, per_device(): kernel = lax.all_gather(own, 'dp', axis=0, tiled=True)  92.9 us
    all_to_all x1, waiting for transfers between devices, per_device(): grad = lax.all_to_all(grad, 'dp', 0, 0, tiled=True)  39.6 us
    all_to_all x1, blocking collectives, per_device(): part = lax.all_to_all(part, 'rows', 0, 0, tiled=True)  22.9 us
    all_to_all x1, waiting for transfers between devices, per_device(): lax.all_to_all(jnp.stack([error] * lax.axis_size('rows')), 'rows', 0, 0)  16.5 us
    all_to_all x1, starting transfers between devices, per_device(): x = lax.all_to_all(latents, 'rows', split_axis=3, concat_axis=1, tiled=True)  6.65 us
    all_to_all x1, starting transfers between devices, per_device(): grad = lax.all_to_all(grad, 'dp', 0, 0, tiled=True)  6.1 us
    unnamed x22, local copies, waits for them, and re-layouts  5.62 us
  transfers between devices with their start and end apart: 4, of which 3 were waited for; matrix products, arithmetic and copies ran while one was open for 3% of the time, Pallas kernels for 0%

profile of v1, /device:TPU:1, one launch (start us, length us, event | category | flops | bytes accessed | tf_op | source)
XLA Modules:
  0.0 220.0 jit_solution(1507548681736204194)
XLA Ops:
  0.6 0.0 copy-start.3
  0.6 1.3 copy.33
  2.0 1.3 reshape.184
  3.3 6.6 %all-to-all-start = ((bf16[8,2,5120]{2,1,0:T(2,128)(2,1)}), bf16[8,2,5120]{2,1,0:T(2,128)(2,1)S(1)}, u32[]{:S(2)}, u32[]{:S(2)}) async-start(bf16[8,2,5120]{2,1,0:T(2,128)(2,1)} %reshape.184), calls=%async_computation | async-start | bytes 327680 | tf_op jit(solution)/shard_map/all_to_all | solution.py:16
  9.9 0.0 copy-done.3
  9.9 0.1 reshape.179
  10.0 92.9 %all-gather = bf16[64,10,720]{2,1,0:T(8,128)(2,1)S(1)} all-gather(bf16[1,10,720]{2,1,0:T(8,128)(2,1)S(1)} %reshape.179), channel_id=1, replica_groups=mesh['dp'=64,'rows'=8] {'dp'}, dimensions={0}, use_global_device_ids=true | all-gather | bytes 936000 | tf_op jit(solution)/shard_map/all_gather | solution.py:15
  103.0 0.6 reshape.180
  103.6 0.0 all-to-all-done
  103.6 0.3 reshape.185
  103.9 0.4 copy.49
  104.4 1.4 pad_slice_fusion.8
  105.8 2.8 %concatenate.31 = bf16[1024,720]{1,0:T(8,128)(2,1)S(1)} concatenate(bf16[1024,80]{1,0:T(8,128)(2,1)} %bitcast.71, bf16[1024,80]{1,0:T(8,128)(2,1)S(1)} %bitcast.65, bf16[1024,80]{1,0:T(8,128)(2,1)} %bitcast.66, bf16[1024,80]{1,0:T(8,128)(2,1)} %bitcast.67, bf16[1024,80]{1,0:T(8,128)(2,1)S(1)} %bitcast.58, bf16[1024,80]{1,0:T(8,128)(2,1)} %bitcast.68, bf16[1024,80]{1,0:T(8,128)(2,1)} %bitcast.69, ...), dimensions={1} | concatenate | bytes 2949120 | tf_op jit(solution)/shard_map/concatenate | solution.py:19
  108.6 0.0 copy-start
  108.6 1.4 convolution_convert_fusion
  110.0 0.0 copy-done
  110.0 0.0 copy-start.4
  110.1 22.9 %all_to_all.51 = bf16[8,128,640]{2,1,0:T(8,128)(2,1)S(1)} all-to-all(bf16[8,128,640]{2,1,0:T(8,128)(2,1)S(1)} %bitcast.61), channel_id=1, replica_groups=mesh['dp'=64,'rows'=8] {'rows'}, dimensions={0} | all-to-all | bytes 2621440 | tf_op jit(solution)/shard_map/all_to_all | solution.py:23
  132.9 0.2 reduce_sum.21
  133.1 0.0 copy-start.2
  133.1 0.0 copy-done.4
  133.2 1.2 stack.3
  134.4 0.0 copy-done.2
  134.4 4.2 %all-to-all-start.2 = ((bf16[8,1,4,32,640]{4,3,2,1,0:T(8,128)(2,1)}), bf16[8,1,4,32,640]{4,3,2,1,0:T(8,128)(2,1)S(1)}, u32[]{:S(2)}, u32[]{:S(2)}) async-start(bf16[8,1,4,32,640]{4,3,2,1,0:T(8,128)(2,1)} %stack.3), calls=%async_computation.2 | async-start | bytes 2621440 | tf_op jit(solution)/shard_map/all_to_all | solution.py:28
  138.6 1.3 copy.38
  139.9 16.5 %all-to-all-done.2 = bf16[8,1,4,32,640]{4,3,2,1,0:T(8,128)(2,1)S(1)} async-done(((bf16[8,1,4,32,640]{4,3,2,1,0:T(8,128)(2,1)}), bf16[8,1,4,32,640]{4,3,2,1,0:T(8,128)(2,1)S(1)}, u32[]{:S(2)}, u32[]{:S(2)}) %all-to-all-start.2) | async-done | bytes 1310752 | tf_op jit(solution)/shard_map/all_to_all | solution.py:28
  156.3 3.3 %convolution_bitcast_fusion = f32[1,32,32,9,80]{4,2,3,1,0:T(8,128)S(1)} fusion(bf16[32,32,640,1]{2,1,3,0:T(8,128)(2,1)S(1)} %bitcast.59, bf16[9,80,640,1]{2,1,0,3:T(8,128)(2,1)} %bitcast.72), kind=kOutput, calls=%fused_computation.9 | convolution fusion | flops 943718400 | bytes 5181440 | tf_op jit(solution)/shard_map/dot_general | solution.py:35
  159.7 0.0 copy-start.1
  159.7 1.3 fusion.9
  161.0 3.7 %all-to-all-start.3 = ((bf16[1,32,32,80]{3,2,0,1:T(8,128)(2,1)}), bf16[1,32,32,80]{3,2,0,1:T(8,128)(2,1)S(1)}, u32[]{:S(2)}, u32[]{:S(2)}) async-start(bf16[1,32,32,80]{3,2,0,1:T(8,128)(2,1)} %fusion.9), calls=%async_computation.3 | async-start | bytes 524288 | tf_op jit(solution)/shard_map/all_to_all | solution.py:43
  164.6 0.0 copy-done.1
  164.6 2.3 %convolution_convert_fusion.1 = bf16[640,720]{0,1:T(8,128)(2,1)} fusion(bf16[1024,640]{1,0:T(8,128)(2,1)S(1)} %bitcast.60, bf16[1024,720]{1,0:T(8,128)(2,1)S(1)} %copy-done.1), kind=kOutput, calls=%fused_computation.11 | convolution fusion | flops 944179200 | bytes 3706880 | tf_op jit(solution)/shard_map/dot_general | solution.py:30
  166.9 1.6 copy.42
  168.5 1.4 reshape.173
  169.8 0.9 all-to-all-done.3
  170.8 6.1 %all-to-all-start.4 = ((bf16[64,10,720]{2,1,0:T(8,128)(2,1)}), bf16[64,10,720]{2,1,0:T(8,128)(2,1)S(1)}, u32[]{:S(2)}, u32[]{:S(2)}) async-start(bf16[64,10,720]{2,1,0:T(8,128)(2,1)} %reshape.173), calls=%async_computation.4 | async-start | bytes 3145728 | tf_op jit(solution)/shard_map/all_to_all | solution.py:32
  176.9 0.0 copy-start.5
  176.9 0.0 copy-start.6
  176.9 0.2 copy.40
  177.1 0.9 all_to_all.44
  178.0 39.6 %all-to-all-done.4 = bf16[64,10,720]{2,1,0:T(8,128)(2,1)S(1)} async-done(((bf16[64,10,720]{2,1,0:T(8,128)(2,1)}), bf16[64,10,720]{2,1,0:T(8,128)(2,1)S(1)}, u32[]{:S(2)}, u32[]{:S(2)}) %all-to-all-start.4) | async-done | bytes 921632 | tf_op jit(solution)/shard_map/all_to_all | solution.py:32
  217.5 0.3 convert_reduce_fusion
  217.8 0.1 div.13
  217.9 0.0 copy-done.5
  217.9 0.0 copy-done.6
  217.9 0.1 copy_subtract_fusion
  218.0 0.6 copy.45
  218.7 0.6 copy.46
  219.3 0.6 copy.47
  (5 shorter events, 0.1 us)
Async XLA Ops:
  0.6 9.3 %copy-start.3 = (f32[9,80,10]{1,2,0:T(8,128)S(1)}, f32[9,80,10]{1,2,0:T(8,128)}, u32[]{:S(2)}) copy-start(f32[9,80,10]{1,2,0:T(8,128)} %param.7) | copy-start | bytes 86404
  3.3 100.3 %all-to-all-start = ((bf16[8,2,5120]{2,1,0:T(2,128)(2,1)}), bf16[8,2,5120]{2,1,0:T(2,128)(2,1)S(1)}, u32[]{:S(2)}, u32[]{:S(2)}) async-start(bf16[8,2,5120]{2,1,0:T(2,128)(2,1)} %reshape.184), calls=%async_computation | async-start | bytes 327680 | tf_op jit(solution)/shard_map/all_to_all | solution.py:16
  108.6 1.4 copy-start
  110.0 23.1 %copy-start.4 = (bf16[1,4,32,640]{3,2,1,0:T(8,128)(2,1)S(1)}, bf16[1,4,32,640]{3,2,1,0:T(8,128)(2,1)}, u32[]{:S(2)}) copy-start(bf16[1,4,32,640]{3,2,1,0:T(8,128)(2,1)} %param.6) | copy-start | bytes 491524
  133.1 1.3 copy-start.2
  134.4 21.9 %all-to-all-start.2 = ((bf16[8,1,4,32,640]{4,3,2,1,0:T(8,128)(2,1)}), bf16[8,1,4,32,640]{4,3,2,1,0:T(8,128)(2,1)S(1)}, u32[]{:S(2)}, u32[]{:S(2)}) async-start(bf16[8,1,4,32,640]{4,3,2,1,0:T(8,128)(2,1)} %stack.3), calls=%async_computation.2 | async-start | bytes 2621440 | tf_op jit(solution)/shard_map/all_to_all | solution.py:28
  159.7 4.9 %copy-start.1 = (bf16[1024,720]{1,0:T(8,128)(2,1)S(1)}, bf16[1024,720]{1,0:T(8,128)(2,1)}, u32[]{:S(2)}) copy-start(bf16[1024,720]{1,0:T(8,128)(2,1)} %copy-done) | copy-start | bytes 4423684
  161.0 9.8 %all-to-all-start.3 = ((bf16[1,32,32,80]{3,2,0,1:T(8,128)(2,1)}), bf16[1,32,32,80]{3,2,0,1:T(8,128)(2,1)S(1)}, u32[]{:S(2)}, u32[]{:S(2)}) async-start(bf16[1,32,32,80]{3,2,0,1:T(8,128)(2,1)} %fusion.9), calls=%async_computation.3 | async-start | bytes 524288 | tf_op jit(solution)/shard_map/all_to_all | solution.py:43
  170.8 46.7 %all-to-all-start.4 = ((bf16[64,10,720]{2,1,0:T(8,128)(2,1)}), bf16[64,10,720]{2,1,0:T(8,128)(2,1)S(1)}, u32[]{:S(2)}, u32[]{:S(2)}) async-start(bf16[64,10,720]{2,1,0:T(8,128)(2,1)} %reshape.173), calls=%async_computation.4 | async-start | bytes 3145728 | tf_op jit(solution)/shard_map/all_to_all | solution.py:32
  176.9 41.0 %copy-start.5 = (f32[9,80,10]{1,2,0:T(8,128)S(1)}, f32[9,80,10]{1,2,0:T(8,128)}, u32[]{:S(2)}) copy-start(f32[9,80,10]{1,2,0:T(8,128)} %param.8) | copy-start | bytes 86404
  176.9 41.0 %copy-start.6 = (f32[9,80,10]{1,2,0:T(8,128)S(1)}, f32[9,80,10]{1,2,0:T(8,128)}, u32[]{:S(2)}) copy-start(f32[9,80,10]{1,2,0:T(8,128)} %param.9) | copy-start | bytes 86404
